TPU v7x, 32 devices: a whole 2x2x4 slice. The times are simulated.
32 devices in a mesh: groups: 2 (over y), tile: 16 (over z, x, core).
Axes of the slice: x: 2, y: 2, z: 4, core: 2. Of those that a mesh axis runs over, the one named last changes fastest.
Arguments:
- features: bfloat16 [1024, 24, 2048], P(('groups', 'tile')), parts along dimension 0, may hold values from 0 to 64, as said below
- aerial_image: bfloat16 [3, 8192, 192], P(None, ('groups', 'tile')), parts along dimension 1, may hold values from -4 to 4
- blocks: int32 [64, 2], P('groups'), parts along dimension 0, may hold values from 0 to 127, as said below
- routes: int32 [64, 1], P('groups'), parts along dimension 0, may hold values from 0 to 15; in each aligned block of 32 rows (0 to 31, 32 to 63, ...) at most 4 rows name the same one
- w_one: bfloat16 [2048, 256], replicated, may hold values from -0.125 to 0.125
- w_depth: bfloat16 [3, 9, 2048], replicated, may hold values from -2 to 2
- w_rates: bfloat16 [3, 2048, 256], replicated, may hold values from -0.125 to 0.125
- w_pool: bfloat16 [2048, 256], replicated, may hold values from -0.125 to 0.125
- w_proj: bfloat16 [1280, 256], replicated, may hold values from -0.15625 to 0.15625
- w_first: bfloat16 [16, 9, 256, 256], P('tile'), may hold values from -0.125 to 0.125
- w_color: bfloat16 [16, 27, 256], P('tile'), may hold values from -1.25 to 1.25
- w_second: bfloat16 [16, 9, 256, 256], P('tile'), may hold values from -0.125 to 0.125
- w_head: bfloat16 [16, 6, 256], P('tile'), may hold values from -0.375 to 0.375
Outputs:
- aspp_features: bfloat16 [1024, 24, 256], P(('groups', 'tile')), parts along dimension 0
- context: float32 [512], P('groups'), parts along dimension 0
- refined: bfloat16 [64, 6, 1024], P(('groups', 'tile')), parts along dimension 0
There are 2 independent parts, one for each index of `groups`. A program takes and returns all parts, laid end to end along the dimension named above; an argument that names none is the same for every part. Nothing has to cross between parts.
Inputs may be any that keep to these rules, and one draw needn't show every extreme that they name: `features`: Non-negative activations. Blocks are distinct; block rows lie below 128 and block columns below 6; no strip of 32 feature rows holds more than 6 blocks and one holds exactly 6. `routes`: at most 4 blocks go to one refiner and one refiner receives exactly 4; every refiner receives one or more.
All inputs are finite; a program needn't handle non-finite values.
Results may differ from a plain program's by a relative error of at most 0.0065.
Values may be sent and summed in bfloat16 or wider, within the bound.
A program may use at most 128 MiB of HBM per device.

v0:
```python
import functools

import jax
import jax.numpy as jnp
import numpy as np
from jax import lax
from jax.experimental import pallas as pl
from jax.experimental.pallas import tpu as pltpu
from jax.sharding import PartitionSpec as P

BLK = 32
CAP = 4
CELLS = 4
RATES = (6, 12, 18)
REACH = 18
CHUNK = 256
F32 = jnp.float32
BF16 = jnp.bfloat16


def split_three(value):
    high = value.astype(BF16)
    rest = value - high.astype(F32)
    mid = rest.astype(BF16)
    low = (rest - mid.astype(F32)).astype(BF16)
    return high, mid, low


def exact_row_dot(row, weights):
    high, mid, low = split_three(row)
    stacked = jnp.concatenate(
        [high.astype(F32), mid.astype(F32), low.astype(F32), jnp.zeros((13, row.shape[1]), F32)], axis=0
    ).astype(BF16)
    product = jnp.dot(stacked, weights, preferred_element_type=F32)
    return product[0:1] + product[1:2] + product[2:3]


def pyramid_kernel(
    tiles, rows, cols, channels, width,
    feat_hbm, w_one_hbm, w_rates_hbm, w_depth_ref, w_pool_hbm, w_proj_hbm, slots_ref, colors_hbm,
    aspp_ref, context_ref, crops_ref, mine_ref,
    feat, w_one, w_rates, w_pool, w_proj, halo, grown, depth, acc, sums, sums_in, crops_out, crops_in, colors_in,
    local_sem, halo_send, halo_recv, sum_send, sum_recv, color_send, color_recv, crop_send, crop_recv,
):
    me = lax.axis_index("tile")
    chunks = channels // CHUNK
    edge = REACH * cols
    cells = rows * cols

    local = [
        pltpu.make_async_copy(source, target, local_sem.at[n])
        for n, (source, target) in enumerate(
            ((feat_hbm, feat), (w_one_hbm, w_one), (w_rates_hbm, w_rates), (w_pool_hbm, w_pool), (w_proj_hbm, w_proj),
             (colors_hbm.at[me], colors_in.at[me]))
        )
    ]
    for copy in local:
        copy.start()

    barrier = pltpu.get_barrier_semaphore()

    def greet(step, carry):
        peer = lax.rem(me + step, tiles)
        pl.semaphore_signal(barrier, inc=1, device_id={"tile": peer}, device_id_type=pl.DeviceIdType.MESH)
        return carry

    lax.fori_loop(1, tiles, greet, 0)
    pl.semaphore_wait(barrier, tiles - 1)

    def halo_copy(side, c):
        lanes = pl.ds(pl.multiple_of(c * CHUNK, CHUNK), CHUNK)
        first = cells - edge if side == 0 else 0
        return pltpu.make_async_remote_copy(
            src_ref=feat_hbm.at[pl.ds(first, edge), lanes],
            dst_ref=halo.at[side, :, lanes],
            send_sem=halo_send.at[side, c],
            recv_sem=halo_recv.at[side, c],
            device_id={"tile": lax.rem(me + 1, tiles) if side == 0 else lax.rem(me + tiles - 1, tiles)},
            device_id_type=pl.DeviceIdType.MESH,
        )

    has_next = me < tiles - 1
    has_prev = me > 0

    def send_halo(c, carry):
        @pl.when(has_next)
        def _():
            halo_copy(0, c).start()

        @pl.when(has_prev)
        def _():
            halo_copy(1, c).start()

        return carry

    lax.fori_loop(0, chunks, send_halo, 0)

    def peer_copy(step, source, target, send, recv):
        return pltpu.make_async_remote_copy(
            src_ref=source, dst_ref=target, send_sem=send.at[step], recv_sem=recv.at[step],
            device_id={"tile": lax.rem(me + step, tiles)}, device_id_type=pl.DeviceIdType.MESH,
        )

    def sum_copy(step):
        return peer_copy(step, sums, sums_in.at[step], sum_send, sum_recv)

    def color_copy(step):
        peer = lax.rem(me + step, tiles)
        return peer_copy(step, colors_hbm.at[peer], colors_in.at[me], color_send, color_recv)

    def crop_copy(step):
        peer = lax.rem(me + step, tiles)
        return peer_copy(step, crops_out.at[peer], crops_in.at[me], crop_send, crop_recv)

    def each_peer(function):
        def body(step, carry):
            function(step)
            return carry

        lax.fori_loop(1, tiles, body, 0)

    local[0].wait()

    def sum_rows(n, totals):
        block = feat[pl.ds(pl.multiple_of(n * 16, 16), 16), :].astype(F32)
        return totals + block[0:8] + block[8:16]

    totals = lax.fori_loop(0, cells // 16, sum_rows, jnp.zeros((8, channels), F32))
    sums[...] = jnp.sum(totals, axis=0, keepdims=True)
    each_peer(lambda step: sum_copy(step).start())
    each_peer(lambda step: color_copy(step).start())

    local[1].wait()
    local[2].wait()
    tall = 256

    @pl.loop(0, cells // tall)
    def _(m):
        span = pl.ds(pl.multiple_of(m * tall, tall), tall)
        acc[0, span, :] = jnp.dot(feat[span, :], w_one[...], preferred_element_type=F32)
        for k in range(3):
            acc[k + 1, span, :] = jnp.zeros((tall, width), F32)

    @pl.when(jnp.logical_not(has_prev))
    def _():
        grown[0:edge, :] = jnp.zeros((edge, CHUNK), F32)

    @pl.when(jnp.logical_not(has_next))
    def _():
        grown[edge + cells :, :] = jnp.zeros((edge, CHUNK), F32)

    def widen(source, start, count, lanes):
        @pl.loop(0, count // 48)
        def _(n):
            grown[pl.ds(pl.multiple_of(start + n * 48, 8), 48), :] = source[
                pl.ds(pl.multiple_of(n * 48, 16), 48), lanes
            ].astype(F32)

    def one_chunk(c, carry):
        lanes = pl.ds(pl.multiple_of(c * CHUNK, CHUNK), CHUNK)
        widen(feat, edge, cells, lanes)

        @pl.when(has_prev)
        def _():
            halo_copy(0, c).wait_recv()
            widen(halo.at[0], 0, edge, lanes)

        @pl.when(has_next)
        def _():
            halo_copy(1, c).wait_recv()
            widen(halo.at[1], edge + cells, edge, lanes)

        for half in range(CHUNK // 128):
            inner = slice(half * 128, half * 128 + 128)
            outer = pl.ds(pl.multiple_of(c * CHUNK + half * 128, 128), 128)
            for k, d in enumerate(RATES):
                taps = [
                    jnp.broadcast_to(w_depth_ref[9 * k + t : 9 * k + t + 1, outer].astype(F32), (8, 128)) for t in range(9)
                ]

                def weigh(parts, column, taps=taps):
                    total = None
                    for i in range(3):
                        tap = jnp.concatenate([taps[3 * i + column]] * (parts[i].shape[0] // 8), axis=0)
                        term = parts[i] * tap
                        total = term if total is None else total + term
                    return total

                @pl.loop(0, rows // 2, unroll=2)
                def _(pair, d=d, weigh=weigh, inner=inner, k=k):
                    results = []
                    for r in range(2):
                        parts = []
                        for i in (-1, 0, 1):
                            start = pl.multiple_of((REACH + i * d + r) * cols + pair * (2 * cols), 8)
                            parts.append(grown[pl.ds(start, cols), inner])
                        low = -(-(cols - d) // 8) * 8
                        high = (d // 8) * 8
                        middle = weigh(parts, 1)
                        left = weigh([p[:low] for p in parts], 0)
                        right = weigh([p[high:] for p in parts], 2)
                        fill = jnp.zeros((d, 128), F32)
                        left = jnp.concatenate([fill, left[: cols - d]], axis=0)
                        right = jnp.concatenate([right[d - high :], fill], axis=0)
                        results.append(jnp.maximum(middle + left + right, 0.0))
                    depth[k, pl.ds(pl.multiple_of(pair * (2 * cols), 16), 2 * cols), inner] = jnp.concatenate(
                        results, axis=0
                    ).astype(BF16)

        for k in range(3):
            @pl.loop(0, cells // tall)
            def _(m, k=k):
                span = pl.ds(pl.multiple_of(m * tall, tall), tall)
                acc[k + 1, span, :] += jnp.dot(depth[k, span, :], w_rates[k, lanes, :], preferred_element_type=F32)

        return carry

    lax.fori_loop(0, chunks, one_chunk, 0)

    each_peer(lambda step: sum_copy(step).wait_recv())

    def add_sums(step, total):
        return total + sums_in[step]

    total = lax.fori_loop(1, tiles, add_sums, sums[...])
    pooled = total / (cells * tiles)
    local[3].wait()
    local[4].wait()
    context = jnp.maximum(exact_row_dot(pooled, w_pool[...]), 0.0)
    context_ref[...] = context
    offset = exact_row_dot(context, w_proj[4 * width :, :])

    @pl.loop(0, cells // tall)
    def _(m):
        span = pl.ds(pl.multiple_of(m * tall, tall), tall)
        blended = jnp.broadcast_to(offset, (tall, width))
        for k in range(4):
            branch = jnp.maximum(acc[k, span, :], 0.0).astype(BF16)
            blended += jnp.dot(branch, w_proj[k * width : (k + 1) * width, :], preferred_element_type=F32)
        aspp_ref[span, :] = jnp.maximum(blended, 0.0).astype(BF16)

    per = CAP * CELLS * CELLS

    def cut(n, carry):
        wanted = slots_ref[pl.ds(pl.multiple_of(n * per, per), per), 0:1]
        chosen = (lax.broadcasted_iota(jnp.int32, (per, cells), 1) == wanted).astype(F32).astype(BF16)
        crops_out[n] = jnp.dot(chosen, aspp_ref[...], preferred_element_type=F32).astype(BF16)
        return carry

    lax.fori_loop(0, tiles, cut, 0)
    crops_in[me] = crops_out[me]
    each_peer(lambda step: crop_copy(step).start())
    local[5].wait()
    each_peer(lambda step: color_copy(step).wait_recv())

    def add_colors(n, total):
        return total + colors_in[n].astype(F32)

    mine_ref[...] = lax.fori_loop(0, tiles, add_colors, jnp.zeros(mine_ref.shape, F32))
    each_peer(lambda step: crop_copy(step).wait_recv())

    def add_crops(n, total):
        return total + crops_in[n].astype(F32)

    crops_ref[...] = lax.fori_loop(0, tiles, add_crops, jnp.zeros(crops_ref.shape, F32)).astype(BF16)

    def drain(step):
        sum_copy(step).wait_send()
        color_copy(step).wait_send()
        crop_copy(step).wait_send()

    each_peer(drain)

    def drain_halo(c, carry):
        @pl.when(has_next)
        def _():
            halo_copy(0, c).wait_send()

        @pl.when(has_prev)
        def _():
            halo_copy(1, c).wait_send()

        return carry

    lax.fori_loop(0, chunks, drain_halo, 0)


def pyramid(tiles, rows, cols, features, w_one, w_rates, w_depth, w_pool, w_proj, slots, colors):
    channels, width = w_one.shape
    cells = rows * cols
    per = CAP * CELLS * CELLS
    chunks = channels // CHUNK
    edge = REACH * cols
    whole = pl.BlockSpec(memory_space=pltpu.VMEM)
    away = pl.BlockSpec(memory_space=pl.ANY)
    dma = pltpu.SemaphoreType.DMA
    return pl.pallas_call(
        functools.partial(pyramid_kernel, tiles, rows, cols, channels, width),
        out_shape=(
            jax.ShapeDtypeStruct((cells, width), BF16),
            jax.ShapeDtypeStruct((1, width), F32),
            jax.ShapeDtypeStruct((per, width), BF16),
            jax.ShapeDtypeStruct((16, 1024), F32),
        ),
        in_specs=[away, away, away, whole, away, away, whole, away],
        out_specs=(whole, whole, whole, whole),
        scratch_shapes=[
            pltpu.VMEM((cells, channels), BF16),
            pltpu.VMEM(w_one.shape, BF16),
            pltpu.VMEM(w_rates.shape, BF16),
            pltpu.VMEM(w_pool.shape, BF16),
            pltpu.VMEM(w_proj.shape, BF16),
            pltpu.VMEM((2, edge, channels), BF16),
            pltpu.VMEM((cells + 2 * edge, CHUNK), F32),
            pltpu.VMEM((3, cells, CHUNK), BF16),
            pltpu.VMEM((4, cells, width), F32),
            pltpu.VMEM((1, channels), F32),
            pltpu.VMEM((tiles, 1, channels), F32),
            pltpu.VMEM((tiles, per, width), BF16),
            pltpu.VMEM((tiles, per, width), BF16),
            pltpu.VMEM((tiles, 16, 1024), BF16),
            dma((6,)),
            dma((2, chunks)),
            dma((2, chunks)),
            dma((tiles,)),
            dma((tiles,)),
            dma((tiles,)),
            dma((tiles,)),
            dma((tiles,)),
            dma((tiles,)),
        ],
        compiler_params=pltpu.CompilerParams(collective_id=0, has_side_effects=True, vmem_limit_bytes=52 << 20),
        name="pyramid",
    )(features.reshape(cells, channels), w_one, w_rates, w_depth.reshape(27, channels), w_pool, w_proj, slots, colors)


def refine_kernel(crops_ref, mine_ref, table_ref, first_ref, color_ref, second_ref, head_ref, out_ref, grid_a, grid_b, patches):
    side, pixels = BLK, BLK * BLK
    width = first_ref.shape[1]
    lane = lax.broadcasted_iota(jnp.int32, (16, pixels), 1)
    row_at, col_at = lane // side, lane % side
    colors = mine_ref[...]
    pieces = []
    for i in (-1, 0, 1):
        for j in (-1, 0, 1):
            moved = colors if i == 0 and j == 0 else pltpu.roll(colors, (-(side * i + j)) % pixels, 1)
            inside = (row_at + i >= 0) & (row_at + i < side) & (col_at + j >= 0) & (col_at + j < side)
            pieces.append(jnp.where(inside, moved, 0.0))
    patches[...] = jnp.concatenate(pieces, axis=0).T.astype(BF16)
    blank = jnp.zeros((side, 3 * width), BF16)
    for grid_ref in (grid_a, grid_b):
        grid_ref[0:side, :] = blank
        grid_ref[side + pixels :, :] = blank
    tall = 256
    col = lax.broadcasted_iota(jnp.int32, (tall, width), 0) % side

    @pl.loop(0, CAP)
    def _(block):
        crop = crops_ref[pl.ds(pl.multiple_of(block * 16, 16), 16), :]

        @pl.loop(0, pixels // tall)
        def _(m):
            at = pl.multiple_of(m * tall, tall)
            for j in range(3):
                up = jnp.dot(table_ref[j, pl.ds(at, tall), :], crop, preferred_element_type=F32)
                grid_a[pl.ds(pl.multiple_of(side + at, side), tall), j * width : (j + 1) * width] = up.astype(BF16)

        @pl.loop(0, pixels // tall)
        def _(m):
            at = pl.multiple_of(m * tall, tall)
            total = jnp.dot(patches[pl.ds(at, tall), :], color_ref[block], preferred_element_type=F32)
            for i in range(3):
                total += jnp.dot(
                    grid_a[pl.ds(pl.multiple_of(at + side * i, side), tall), :],
                    first_ref[3 * width * i : 3 * width * (i + 1), :],
                    preferred_element_type=F32,
                )
            total = jnp.maximum(total, 0.0)
            before = jnp.where(col == 0, 0.0, pltpu.roll(total, 1, 0))
            after = jnp.where(col == side - 1, 0.0, pltpu.roll(total, tall - 1, 0))
            inner = pl.ds(pl.multiple_of(side + at, side), tall)
            grid_b[inner, 0:width] = before.astype(BF16)
            grid_b[inner, width : 2 * width] = total.astype(BF16)
            grid_b[inner, 2 * width :] = after.astype(BF16)

        @pl.loop(0, pixels // tall)
        def _(m):
            at = pl.multiple_of(m * tall, tall)
            total = jnp.zeros((tall, width), F32)
            for i in range(3):
                total += jnp.dot(
                    grid_b[pl.ds(pl.multiple_of(at + side * i, side), tall), :],
                    second_ref[3 * width * i : 3 * width * (i + 1), :],
                    preferred_element_type=F32,
                )
            total = jnp.maximum(total, 0.0).astype(BF16)
            scores = lax.dot_general(
                head_ref[...], total, (((1,), (1,)), ((), ())), preferred_element_type=F32
            )
            out_ref[block, :, pl.ds(at, tall)] = scores.astype(BF16)


def upsample_tables():
    pixels = np.arange(BLK, dtype=np.float32)
    source = np.clip((pixels + 0.5) / 8.0 - 0.5, 0.0, CELLS - 1.0)
    table = np.maximum(1.0 - np.abs(source[:, None] - np.arange(CELLS, dtype=np.float32)[None, :]), 0.0)
    tables = []
    for j in (-1, 0, 1):
        moved = np.zeros_like(table)
        for q in range(BLK):
            if 0 <= q + j < BLK:
                moved[q] = table[q + j]
        tables.append((table[:, None, :, None] * moved[None, :, None, :]).reshape(BLK * BLK, CELLS * CELLS))
    return np.stack(tables)


def refine(crops, mine, w_first, w_color, w_second, w_head):
    width = w_first.shape[1]
    classes = w_head.shape[0]
    placed = jnp.zeros((CAP, 9, CAP, 4, width), BF16)
    taps = w_color.reshape(9, 3, width)
    for slot in range(CAP):
        placed = placed.at[slot, :, slot, :3, :].set(taps)
    head = jnp.pad(w_head, ((0, 16 - classes), (0, 0)))
    whole = pl.BlockSpec(memory_space=pltpu.VMEM)
    pixels = BLK * BLK
    scores = pl.pallas_call(
        refine_kernel,
        out_shape=jax.ShapeDtypeStruct((CAP, 16, pixels), BF16),
        in_specs=[whole] * 7,
        out_specs=whole,
        scratch_shapes=[
            pltpu.VMEM((pixels + 2 * BLK, 3 * width), BF16),
            pltpu.VMEM((pixels + 2 * BLK, 3 * width), BF16),
            pltpu.VMEM((pixels, 144), BF16),
        ],
        compiler_params=pltpu.CompilerParams(vmem_limit_bytes=40 << 20),
        name="refine",
    )(
        crops,
        mine,
        jnp.asarray(upsample_tables(), BF16),
        w_first.reshape(9 * width, width),
        placed.reshape(CAP, 144, width),
        w_second.reshape(9 * width, width),
        head,
    )
    return scores[:, :classes, :]


def shards(
    tiles,
    features,
    aerial_image,
    blocks,
    routes,
    w_one,
    w_depth,
    w_rates,
    w_pool,
    w_proj,
    w_first,
    w_color,
    w_second,
    w_head,
):
    rows, cols, channels = features.shape
    width = w_one.shape[1]
    me = lax.axis_index("tile")
    count = blocks.shape[0]
    per_holder = count // tiles
    strip_blocks = rows * 8 // BLK
    across = cols // CELLS
    block_row, block_col, experts = blocks[:, 0], blocks[:, 1], routes[:, 0]
    owners = block_row // strip_blocks
    positions = jnp.arange(count, dtype=jnp.int32)
    earlier = positions[None, :] < positions[:, None]
    rank = jnp.sum(earlier & (experts[:, None] == experts[None, :]), axis=1)
    slot_of = experts * CAP + rank
    local_row = block_row - owners * strip_blocks
    place = local_row * across + block_col
    mine_here = owners == me
    slot_hit = (slot_of[None, :] == jnp.arange(tiles * CAP, dtype=jnp.int32)[:, None]) & mine_here[None, :]
    slot_place = jnp.max(jnp.where(slot_hit, place[None, :], -1), axis=1)
    pieces = aerial_image.reshape(3, strip_blocks, BLK, across, BLK).transpose(1, 3, 0, 2, 4)
    pieces = pieces.reshape(strip_blocks * across, 3 * BLK * BLK)
    chosen = (slot_place[:, None] == jnp.arange(strip_blocks * across, dtype=jnp.int32)[None, :]).astype(BF16)
    colors = jnp.dot(chosen, pieces, preferred_element_type=F32).astype(BF16).reshape(tiles, CAP, 3, BLK * BLK)
    colors = jnp.pad(colors, ((0, 0), (0, 0), (0, 1), (0, 0))).reshape(tiles, CAP * 4, BLK * BLK)
    cell = jnp.arange(CELLS * CELLS, dtype=jnp.int32)
    top = slot_place // across * CELLS
    left = slot_place % across * CELLS
    cell_at = (top[:, None] + cell[None, :] // CELLS) * cols + left[:, None] + cell[None, :] % CELLS
    cell_at = jnp.where(slot_place[:, None] >= 0, cell_at, -1).reshape(tiles * CAP * CELLS * CELLS, 1)
    aspp, context, crops, mine = pyramid(
        tiles, rows, cols, features, w_one, w_rates, w_depth, w_pool, w_proj, cell_at, colors
    )
    result = refine(crops, mine, w_first[0], w_color[0], w_second[0], w_head[0])
    pick = ((experts == me)[:, None] & (rank[:, None] == jnp.arange(CAP)[None, :])).astype(BF16)
    send_back = jnp.dot(pick, result.reshape(CAP, -1), preferred_element_type=F32).astype(BF16)
    arrived = lax.all_to_all(
        send_back.reshape(tiles, per_holder, result.shape[1], result.shape[2]), "tile", split_axis=0, concat_axis=0, tiled=True
    )
    refined = jnp.sum(arrived, axis=0, dtype=F32).astype(BF16)
    return aspp.reshape(rows, cols, width), context.reshape(width), refined


def solution(mesh):
    return jax.shard_map(
        functools.partial(shards, mesh.shape["tile"]),
        mesh=mesh,
        in_specs=(
            P(("groups", "tile"), None, None),
            P(None, ("groups", "tile"), None),
            P("groups", None),
            P("groups", None),
            P(),
            P(),
            P(),
            P(),
            P(),
            P("tile", None, None, None),
            P("tile", None, None),
            P("tile", None, None, None),
            P("tile", None, None),
        ),
        out_specs=(
            P(("groups", "tile"), None, None),
            P("groups"),
            P(("groups", "tile"), None, None),
        ),
        check_vma=False,
    )
```

profile of v0, /device:TPU:15, one launch (start us, length us, event | category | flops | bytes accessed | tf_op | source)
XLA Modules:
  0.0 129.3 jit_solution(16541281261783038784)
XLA Ops:
  0.6 0.9 convert_reduce_fusion
  1.5 0.7 broadcast_compare_fusion.1
  2.2 0.8 bitcast_add_fusion
  3.1 0.7 compare_bitcast_fusion
  3.9 0.3 reshape.416.slots_ref
  4.2 1.7 %reshape.404 = bf16[3,8,32,6,32]{2,1,4,3,0:T(8,128)(2,1)S(1)} reshape(bf16[3,256,192]{1,2,0:T(8,128)(2,1)} %param.23) | data formatting | bytes 589824 | tf_op jit(solution)/shard_map/reshape | solution.py:485
  5.9 0.9 copy.40
  6.9 1.2 reshape.405
  8.1 0.3 convolution_convert_fusion.1
  8.4 0.6 reshape.406
  9.0 0.3 pad.25
  9.4 0.5 copy-done.3
  10.2 0.2 scatter.15
  10.4 0.2 scatter.16
  10.8 74.3 %pyramid.1 = (bf16[768,256]{1,0:T(8,128)(2,1)S(1)}, f32[1,256]{1,0:T(1,128)S(1)}, bf16[64,256]{1,0:T(8,128)(2,1)S(1)}, f32[16,1024]{1,0:T(8,128)S(1)}) custom-call(bf16[768,2048]{1,0:T(8,128)(2,1)} %bitcast.45, bf16[2048,256]{1,0:T(8,128)(2,1)} %w_one_hbm.1, bf16[3,2048,256]{2,1,0:T(8,128)(2,1)} %w_rates_hbm.1, bf16[27,2048]{1,0:T(8,128)(2,1)S(1)} %reshape.403.w_depth_ref, ...), custom_call_target="tpu_custom_call" | custom-call | tf_op jit(solution)/shard_map/pyramid/pallas_call | solution.py:297
  85.2 22.5 %refine.1 = bf16[4,16,1024]{2,1,0:T(8,128)(2,1)S(1)} custom-call(bf16[64,256]{1,0:T(8,128)(2,1)S(1)} %get-tuple-element.57.crops_ref, f32[16,1024]{1,0:T(8,128)S(1)} %get-tuple-element.58.mine_ref, bf16[3,1024,16]{2,1,0:T(8,128)(2,1)S(1)} %copy-done.2, bf16[2304,256]{1,0:T(8,128)(2,1)S(1)} %bitcast.40, bf16[4,144,256]{2,1,0:T(8,128)(2,1)S(1)} %reshape.411.color_ref, ...), custom_call_target="tpu_custom_call" | custom-call | tf_op jit(solution)/shard_map/refine/pallas_call | solution.py:427
  107.8 0.3 convolution_convert_fusion
  108.1 0.5 reshape.413
  108.6 1.2 copy.46
  109.8 6.5 %all-to-all-start = ((bf16[16,2,6,1024]{3,1,2,0:T(2,128)(2,1)}), bf16[16,2,6,1024]{3,1,2,0:T(2,128)(2,1)S(1)}, u32[]{:S(2)}, u32[]{:S(2)}) async-start(bf16[16,2,6,1024]{3,1,2,0:T(2,128)(2,1)} %copy.46), calls=%async_computation | async-start | bytes 786432 | tf_op jit(solution)/shard_map/all_to_all | solution.py:501
  116.3 10.8 %all-to-all-done = bf16[16,2,6,1024]{3,1,2,0:T(2,128)(2,1)S(1)} async-done(((bf16[16,2,6,1024]{3,1,2,0:T(2,128)(2,1)}), bf16[16,2,6,1024]{3,1,2,0:T(2,128)(2,1)S(1)}, u32[]{:S(2)}, u32[]{:S(2)}) %all-to-all-start) | async-done | bytes 393248 | tf_op jit(solution)/shard_map/all_to_all | solution.py:501
  127.0 0.9 reduce_sum.22
  128.0 0.7 copy.56
  128.7 0.6 copy.57
  (26 shorter events, 0.9 us)
Async XLA Ops:
  9.0 0.9 copy-start.3
  9.0 1.0 copy-start.4
  9.3 1.5 %copy-start.5 = (bf16[1,6,256]{2,1,0:T(8,128)(2,1)S(1)}, bf16[1,6,256]{2,1,0:T(8,128)(2,1)}, u32[]{:S(2)}) copy-start(bf16[1,6,256]{2,1,0:T(8,128)(2,1)} %param.34) | copy-start | bytes 9220
  10.8 74.4 %copy-start = (bf16[1,9,256,256]{3,2,1,0:T(8,128)(2,1)S(1)}, bf16[1,9,256,256]{3,2,1,0:T(8,128)(2,1)}, u32[]{:S(2)}) copy-start(bf16[1,9,256,256]{3,2,1,0:T(8,128)(2,1)} %param.31) | copy-start | bytes 3538948
  10.8 74.4 %copy-start.1 = (bf16[1,9,256,256]{3,2,1,0:T(8,128)(2,1)S(1)}, bf16[1,9,256,256]{3,2,1,0:T(8,128)(2,1)}, u32[]{:S(2)}) copy-start(bf16[1,9,256,256]{3,2,1,0:T(8,128)(2,1)} %param.33) | copy-start | bytes 3538948
  10.8 74.4 %copy-start.2 = (bf16[3,1024,16]{2,1,0:T(8,128)(2,1)S(1)}, bf16[3,1024,16]{2,1,0:T(8,128)(2,1)}, u32[]{:S(2)}) copy-start(bf16[3,1024,16]{2,1,0:T(8,128)(2,1)} %constant.214.clone.table_ref) | copy-start | bytes 294916
  109.8 17.2 %all-to-all-start = ((bf16[16,2,6,1024]{3,1,2,0:T(2,128)(2,1)}), bf16[16,2,6,1024]{3,1,2,0:T(2,128)(2,1)S(1)}, u32[]{:S(2)}, u32[]{:S(2)}) async-start(bf16[16,2,6,1024]{3,1,2,0:T(2,128)(2,1)} %copy.46), calls=%async_computation | async-start | bytes 786432 | tf_op jit(solution)/shard_map/all_to_all | solution.py:501
where the time goes:
time: 132 us; the launch traced here: 129 us
  Pallas kernels  96.9 us (73%)
  waiting for transfers between devices  10.8 us (8%)
  local copies, waits for them, and re-layouts  9.48 us (7%)
  starting transfers between devices  6.47 us (5%)
  other arithmetic  4.18 us (3%)
    pallas_call x1, Pallas kernels, pyramid(): pl.pallas_call(functools.partial(pyramid_kernel, tiles, rows, cols, chann...  74.3 us
    pallas_call x1, Pallas kernels, refine(): pl.pallas_call(refine_kernel, out_shape=jax.ShapeDtypeStruct((CAP, 16, pi...  22.5 us
    all_to_all x1, waiting for transfers between devices, shards(): lax.all_to_all(send_back.reshape(tiles, per_holder, result.shape[1], resu...  10.8 us
    all_to_all x1, starting transfers between devices, shards(): lax.all_to_all(send_back.reshape(tiles, per_holder, result.shape[1], resu...  6.47 us
    reshape x2, local copies, waits for them, and re-layouts, shards(): aerial_image.reshape(3, strip_blocks, BLK, across, BLK)  2.67 us
  transfers between devices with their start and end apart: 1, of which 1 were waited for; matrix products, arithmetic and copies ran while one was open for 0% of the time, Pallas kernels for 0%

commit v1 on v0

v1 whole, which is shorter than its diff:
```python
import functools

import jax
import jax.numpy as jnp
import numpy as np
from jax import lax
from jax.experimental import pallas as pl
from jax.experimental.pallas import tpu as pltpu
from jax.sharding import PartitionSpec as P

BLK = 32
CAP = 4
CELLS = 4
RATES = (6, 12, 18)
REACH = 18
CHUNK = 256
F32 = jnp.float32
BF16 = jnp.bfloat16


def split_three(value):
    high = value.astype(BF16)
    rest = value - high.astype(F32)
    mid = rest.astype(BF16)
    low = (rest - mid.astype(F32)).astype(BF16)
    return high, mid, low


def exact_row_dot(row, weights):
    high, mid, low = split_three(row)
    stacked = jnp.concatenate(
        [high.astype(F32), mid.astype(F32), low.astype(F32), jnp.zeros((13, row.shape[1]), F32)], axis=0
    ).astype(BF16)
    product = jnp.dot(stacked, weights, preferred_element_type=F32)
    return product[0:1] + product[1:2] + product[2:3]


def pyramid_kernel(
    tiles, rows, cols, channels, width,
    feat_hbm, w_one_hbm, w_rates_hbm, w_depth_ref, w_pool_hbm, w_proj_hbm, image_hbm, first_hbm, second_hbm,
    color_ref, head_ref, table_ref, blocks_ref, routes_ref,
    aspp_ref, context_ref, refined_ref,
    image, first, second, crops_ref, mine_ref, grid_a, grid_b, patches, scores, back_out, back_in, colors_out, back_send, back_recv,
    feat, w_one, w_rates, w_pool, w_proj, halo, grown, depth, acc, sums, sums_in, crops_out, crops_in, colors_in,
    local_sem, halo_send, halo_recv, sum_send, sum_recv, color_send, color_recv, crop_send, crop_recv,
):
    me = lax.axis_index("tile")
    chunks = channels // CHUNK
    edge = REACH * cols
    cells = rows * cols
    count = routes_ref.shape[1]
    held = count // tiles * 8

    local = [
        pltpu.make_async_copy(source, target, local_sem.at[n])
        for n, (source, target) in enumerate(
            ((feat_hbm, feat), (w_one_hbm, w_one), (w_rates_hbm, w_rates), (w_pool_hbm, w_pool), (w_proj_hbm, w_proj),
             (image_hbm, image), (first_hbm, first), (second_hbm, second))
        )
    ]
    for copy in local:
        copy.start()

    barrier = pltpu.get_barrier_semaphore()

    def greet(step, carry):
        peer = lax.rem(me + step, tiles)
        pl.semaphore_signal(barrier, inc=1, device_id={"tile": peer}, device_id_type=pl.DeviceIdType.MESH)
        return carry

    lax.fori_loop(1, tiles, greet, 0)
    pl.semaphore_wait(barrier, tiles - 1)

    def halo_copy(side, c):
        lanes = pl.ds(pl.multiple_of(c * CHUNK, CHUNK), CHUNK)
        first = cells - edge if side == 0 else 0
        return pltpu.make_async_remote_copy(
            src_ref=feat_hbm.at[pl.ds(first, edge), lanes],
            dst_ref=halo.at[side, :, lanes],
            send_sem=halo_send.at[side, c],
            recv_sem=halo_recv.at[side, c],
            device_id={"tile": lax.rem(me + 1, tiles) if side == 0 else lax.rem(me + tiles - 1, tiles)},
            device_id_type=pl.DeviceIdType.MESH,
        )

    has_next = me < tiles - 1
    has_prev = me > 0

    def send_halo(c, carry):
        @pl.when(has_next)
        def _():
            halo_copy(0, c).start()

        @pl.when(has_prev)
        def _():
            halo_copy(1, c).start()

        return carry

    lax.fori_loop(0, chunks, send_halo, 0)

    def peer_copy(step, source, target, send, recv):
        return pltpu.make_async_remote_copy(
            src_ref=source, dst_ref=target, send_sem=send.at[step], recv_sem=recv.at[step],
            device_id={"tile": lax.rem(me + step, tiles)}, device_id_type=pl.DeviceIdType.MESH,
        )

    def sum_copy(step):
        return peer_copy(step, sums, sums_in.at[step], sum_send, sum_recv)

    def color_copy(step):
        peer = lax.rem(me + step, tiles)
        return peer_copy(step, colors_out.at[pl.ds(pl.multiple_of(peer * 16, 16), 16)], colors_in.at[me], color_send, color_recv)

    def crop_copy(step):
        peer = lax.rem(me + step, tiles)
        return peer_copy(step, crops_out.at[peer], crops_in.at[me], crop_send, crop_recv)

    def back_copy(step):
        peer = lax.rem(me + step, tiles)
        return peer_copy(
            step, back_out.at[pl.ds(pl.multiple_of(peer * held, held), held)], back_in.at[me], back_send, back_recv
        )

    def each_peer(function):
        def body(step, carry):
            function(step)
            return carry

        lax.fori_loop(1, tiles, body, 0)

    local[0].wait()

    def sum_rows(n, totals):
        block = feat[pl.ds(pl.multiple_of(n * 16, 16), 16), :].astype(F32)
        return totals + block[0:8] + block[8:16]

    totals = lax.fori_loop(0, cells // 16, sum_rows, jnp.zeros((8, channels), F32))
    sums[...] = jnp.sum(totals, axis=0, keepdims=True)
    each_peer(lambda step: sum_copy(step).start())

    local[1].wait()
    local[2].wait()
    tall = 256

    @pl.loop(0, cells // tall)
    def _(m):
        span = pl.ds(pl.multiple_of(m * tall, tall), tall)
        acc[0, span, :] = jnp.dot(feat[span, :], w_one[...], preferred_element_type=F32)
        for k in range(3):
            acc[k + 1, span, :] = jnp.zeros((tall, width), F32)

    @pl.when(jnp.logical_not(has_prev))
    def _():
        grown[0:edge, :] = jnp.zeros((edge, CHUNK), F32)

    @pl.when(jnp.logical_not(has_next))
    def _():
        grown[edge + cells :, :] = jnp.zeros((edge, CHUNK), F32)

    def widen(source, start, count, lanes):
        @pl.loop(0, count // 48)
        def _(n):
            grown[pl.ds(pl.multiple_of(start + n * 48, 8), 48), :] = source[
                pl.ds(pl.multiple_of(n * 48, 16), 48), lanes
            ].astype(F32)

    experts = routes_ref[...].astype(F32)
    square = (count, count)
    down, over = lax.broadcasted_iota(jnp.int32, square, 0), lax.broadcasted_iota(jnp.int32, square, 1)
    spread = jnp.broadcast_to(experts, square)
    upright = jnp.sum(jnp.where(down == over, spread, 0.0), axis=1, keepdims=True)
    rank = jnp.sum(jnp.where((upright == spread) & (down < over), 1.0, 0.0), axis=0, keepdims=True)
    slot_of = experts * CAP + rank
    strip_blocks = rows // CELLS
    local_row = blocks_ref[0:1, :].astype(F32) - lax.convert_element_type(me * strip_blocks, F32)
    is_mine = (local_row >= 0) & (local_row < strip_blocks)
    base = jnp.where(is_mine, local_row * (CELLS * cols) + blocks_ref[1:2, :].astype(F32) * CELLS, -1e6)
    to_me = jnp.where(experts == lax.convert_element_type(me, F32), rank, -1.0)

    def lookup(slot, values, fill):
        shape = (slot.shape[0], count)
        hit = jnp.broadcast_to(slot, shape) == jnp.broadcast_to(slot_of, shape)
        return jnp.max(jnp.where(hit, jnp.broadcast_to(values, shape), fill), axis=1, keepdims=True)

    local[5].wait()
    parts_high = image.shape[0]
    across = parts_high // 3
    group = 256
    line = lax.broadcasted_iota(jnp.int32, (group, 1), 0)
    lane = lax.broadcasted_iota(jnp.int32, (1, BLK * BLK), 1)
    source = lax.broadcasted_iota(jnp.int32, (1, parts_high), 1)
    source_channel = (source >= across).astype(jnp.int32) + (source >= 2 * across).astype(jnp.int32)
    source_block = (source - source_channel * across) // BLK
    deep = lax.broadcasted_iota(jnp.int32, (parts_high, 1), 0)
    keep = ((deep & (BLK - 1)) == (lane & (BLK - 1)))
    tall_rows = image.shape[1]
    image_row = lax.broadcasted_iota(jnp.int32, (tall_rows, 1), 0)
    colors_out[...] = jnp.zeros(colors_out.shape, BF16)

    @pl.loop(0, strip_blocks)
    def _(at):
        select = (image_row == at * BLK + (lane >> 5)).astype(F32).astype(BF16)
        strips = jnp.dot(image[...], select, preferred_element_type=F32)
        strips = jnp.where(keep, strips, 0.0).astype(BF16)

        @pl.loop(0, tiles * 16 // group)
        def _(n):
            row = line + n * group
            found = lookup((row >> 2).astype(F32), base, -1e6)
            wanted = (at * (CELLS * cols) + source_block * CELLS).astype(F32)
            chosen = ((found == wanted) & ((row & 3) == source_channel)).astype(F32).astype(BF16)
            span = pl.ds(pl.multiple_of(n * group, group), group)
            colors_out[span, :] += jnp.dot(chosen, strips, preferred_element_type=F32).astype(BF16)

    def one_chunk(c, carry):
        @pl.when(c == chunks - 2)
        def _():
            each_peer(lambda step: color_copy(step).start())

        lanes = pl.ds(pl.multiple_of(c * CHUNK, CHUNK), CHUNK)
        widen(feat, edge, cells, lanes)

        @pl.when(has_prev)
        def _():
            halo_copy(0, c).wait_recv()
            widen(halo.at[0], 0, edge, lanes)

        @pl.when(has_next)
        def _():
            halo_copy(1, c).wait_recv()
            widen(halo.at[1], edge + cells, edge, lanes)

        for half in range(CHUNK // 128):
            inner = slice(half * 128, half * 128 + 128)
            outer = pl.ds(pl.multiple_of(c * CHUNK + half * 128, 128), 128)
            for k, d in enumerate(RATES):
                taps = [
                    jnp.broadcast_to(w_depth_ref[t, k : k + 1, outer].astype(F32), (8, 128)) for t in range(9)
                ]

                def weigh(parts, column, taps=taps):
                    total = None
                    for i in range(3):
                        tap = jnp.concatenate([taps[3 * i + column]] * (parts[i].shape[0] // 8), axis=0)
                        term = parts[i] * tap
                        total = term if total is None else total + term
                    return total

                @pl.loop(0, rows // 2, unroll=2)
                def _(pair, d=d, weigh=weigh, inner=inner, k=k):
                    results = []
                    for r in range(2):
                        parts = []
                        for i in (-1, 0, 1):
                            start = pl.multiple_of((REACH + i * d + r) * cols + pair * (2 * cols), 8)
                            parts.append(grown[pl.ds(start, cols), inner])
                        low = -(-(cols - d) // 8) * 8
                        high = (d // 8) * 8
                        middle = weigh(parts, 1)
                        left = weigh([p[:low] for p in parts], 0)
                        right = weigh([p[high:] for p in parts], 2)
                        fill = jnp.zeros((d, 128), F32)
                        left = jnp.concatenate([fill, left[: cols - d]], axis=0)
                        right = jnp.concatenate([right[d - high :], fill], axis=0)
                        results.append(jnp.maximum(middle + left + right, 0.0))
                    depth[k, pl.ds(pl.multiple_of(pair * (2 * cols), 16), 2 * cols), inner] = jnp.concatenate(
                        results, axis=0
                    ).astype(BF16)

        for k in range(3):
            @pl.loop(0, cells // tall)
            def _(m, k=k):
                span = pl.ds(pl.multiple_of(m * tall, tall), tall)
                acc[k + 1, span, :] += jnp.dot(depth[k, span, :], w_rates[k, lanes, :], preferred_element_type=F32)

        return carry

    lax.fori_loop(0, chunks, one_chunk, 0)

    each_peer(lambda step: sum_copy(step).wait_recv())

    def add_sums(step, total):
        return total + sums_in[step]

    total = lax.fori_loop(1, tiles, add_sums, sums[...])
    pooled = total / (cells * tiles)
    local[3].wait()
    local[4].wait()
    context = jnp.maximum(exact_row_dot(pooled, w_pool[...]), 0.0)
    context_ref[...] = context
    offset = exact_row_dot(context, w_proj[4 * width :, :])

    @pl.loop(0, cells // tall)
    def _(m):
        span = pl.ds(pl.multiple_of(m * tall, tall), tall)
        blended = jnp.broadcast_to(offset, (tall, width))
        for k in range(4):
            branch = jnp.maximum(acc[k, span, :], 0.0).astype(BF16)
            blended += jnp.dot(branch, w_proj[k * width : (k + 1) * width, :], preferred_element_type=F32)
        aspp_ref[span, :] = jnp.maximum(blended, 0.0).astype(BF16)

    per = CAP * CELLS * CELLS
    cell_row = lax.broadcasted_iota(jnp.int32, (per, 1), 0)

    def cut(n, carry):
        slot = (n * CAP + (cell_row >> 4)).astype(F32)
        wanted = lookup(slot, base, -1e6) + (((cell_row >> 2) & 3) * cols + (cell_row & 3)).astype(F32)
        chosen = (lax.broadcasted_iota(jnp.int32, (per, cells), 1).astype(F32) == wanted).astype(F32).astype(BF16)
        crops_out[n] = jnp.dot(chosen, aspp_ref[...], preferred_element_type=F32).astype(BF16)
        return carry

    lax.fori_loop(0, tiles, cut, 0)
    crops_in[me] = crops_out[me]
    each_peer(lambda step: crop_copy(step).start())
    colors_in[me] = colors_out[pl.ds(pl.multiple_of(me * 16, 16), 16), :]
    each_peer(lambda step: color_copy(step).wait_recv())

    def add_colors(n, total):
        return total + colors_in[n].astype(F32)

    mine_ref[...] = lax.fori_loop(0, tiles, add_colors, jnp.zeros(mine_ref.shape, F32))
    side, pixels = BLK, BLK * BLK
    wide = lax.broadcasted_iota(jnp.int32, (16, pixels), 1)
    row_at, col_at = wide >> 5, wide & (side - 1)
    colors = mine_ref[...]
    pieces = []
    for i in (-1, 0, 1):
        for j in (-1, 0, 1):
            moved = colors if i == 0 and j == 0 else pltpu.roll(colors, (-(side * i + j)) % pixels, 1)
            inside = (row_at + i >= 0) & (row_at + i < side) & (col_at + j >= 0) & (col_at + j < side)
            pieces.append(jnp.where(inside, moved, 0.0))
    patches[...] = jnp.concatenate(pieces, axis=0).T.astype(BF16)
    blank = jnp.zeros((side, 3 * width), BF16)
    for grid_ref in (grid_a, grid_b):
        grid_ref[0:side, :] = blank
        grid_ref[side + pixels :, :] = blank
    tall = 512
    local[6].wait()
    local[7].wait()
    scores[...] = jnp.zeros(scores.shape, F32)
    col = lax.broadcasted_iota(jnp.int32, (tall, width), 0) & (side - 1)

    each_peer(lambda step: crop_copy(step).wait_recv())

    def add_crops(n, total):
        return total + crops_in[n].astype(F32)

    crops_ref[...] = lax.fori_loop(0, tiles, add_crops, jnp.zeros(crops_ref.shape, F32)).astype(BF16)

    @pl.loop(0, CAP)
    def _(block):
        tap_row = lax.broadcasted_iota(jnp.int32, (144, 27), 0)
        channel = (tap_row & 15) - block * 4
        wanted_tap = (tap_row >> 4) * 3 + channel
        spread_taps = (channel >= 0) & (channel < 3) & (wanted_tap == lax.broadcasted_iota(jnp.int32, (144, 27), 1))
        tap_weights = jnp.dot(
            spread_taps.astype(F32).astype(BF16), color_ref[...], preferred_element_type=F32
        ).astype(BF16)
        crop = crops_ref[pl.ds(pl.multiple_of(block * 16, 16), 16), :]

        @pl.loop(0, pixels // tall)
        def _(m):
            at = pl.multiple_of(m * tall, tall)
            for j in range(3):
                up = jnp.dot(table_ref[j, pl.ds(at, tall), :], crop, preferred_element_type=F32)
                grid_a[pl.ds(pl.multiple_of(side + at, side), tall), j * width : (j + 1) * width] = up.astype(BF16)

        @pl.loop(0, pixels // tall)
        def _(m):
            at = pl.multiple_of(m * tall, tall)
            total = jnp.dot(patches[pl.ds(at, tall), :], tap_weights, preferred_element_type=F32)
            for i in range(3):
                total += jnp.dot(
                    grid_a[pl.ds(pl.multiple_of(at + side * i, side), tall), :],
                    first[3 * width * i : 3 * width * (i + 1), :],
                    preferred_element_type=F32,
                )
            total = jnp.maximum(total, 0.0)
            before = jnp.where(col == 0, 0.0, pltpu.roll(total, 1, 0))
            after = jnp.where(col == side - 1, 0.0, pltpu.roll(total, tall - 1, 0))
            inner = pl.ds(pl.multiple_of(side + at, side), tall)
            grid_b[inner, 0:width] = before.astype(BF16)
            grid_b[inner, width : 2 * width] = total.astype(BF16)
            grid_b[inner, 2 * width :] = after.astype(BF16)

        @pl.loop(0, pixels // tall)
        def _(m):
            at = pl.multiple_of(m * tall, tall)
            total = jnp.zeros((tall, width), F32)
            for i in range(3):
                total += jnp.dot(
                    grid_b[pl.ds(pl.multiple_of(at + side * i, side), tall), :],
                    second[3 * width * i : 3 * width * (i + 1), :],
                    preferred_element_type=F32,
                )
            total = jnp.maximum(total, 0.0).astype(BF16)
            found = lax.dot_general(
                head_ref[...], total, (((1,), (1,)), ((), ())), preferred_element_type=F32
            )
            scores[pl.ds(pl.multiple_of(block * 8, 8), head_ref.shape[0]), pl.ds(at, tall)] = found

    finished = scores[...].astype(BF16)
    step_rows = min(tiles * held, 256)
    item = lax.broadcasted_iota(jnp.int32, (step_rows, 1), 0)
    given = lax.broadcasted_iota(jnp.int32, (step_rows, 8 * CAP), 1)
    listed = lax.broadcasted_iota(jnp.int32, (step_rows, count), 1)

    @pl.loop(0, tiles * held // step_rows)
    def _(n):
        number = item + n * step_rows
        slot = jnp.max(
            jnp.where(listed == (number >> 3), jnp.broadcast_to(to_me, (step_rows, count)), -1.0), axis=1, keepdims=True
        )
        pick = ((given >> 3).astype(F32) == slot) & ((given & 7) == (number & 7))
        back_out[pl.ds(pl.multiple_of(n * step_rows, step_rows), step_rows), :] = jnp.dot(
            pick.astype(F32).astype(BF16), finished, preferred_element_type=F32
        ).astype(BF16)

    each_peer(lambda step: back_copy(step).start())
    back_in[me] = back_out[pl.ds(pl.multiple_of(me * held, held), held), :]
    each_peer(lambda step: back_copy(step).wait_recv())

    def add_back(n, total):
        return total + back_in[n].astype(F32)

    refined_ref[...] = lax.fori_loop(0, tiles, add_back, jnp.zeros(refined_ref.shape, F32)).astype(BF16)

    def drain(step):
        sum_copy(step).wait_send()
        color_copy(step).wait_send()
        crop_copy(step).wait_send()
        back_copy(step).wait_send()

    each_peer(drain)

    def drain_halo(c, carry):
        @pl.when(has_next)
        def _():
            halo_copy(0, c).wait_send()

        @pl.when(has_prev)
        def _():
            halo_copy(1, c).wait_send()

        return carry

    lax.fori_loop(0, chunks, drain_halo, 0)


def upsample_tables():
    pixels = np.arange(BLK, dtype=np.float32)
    source = np.clip((pixels + 0.5) / 8.0 - 0.5, 0.0, CELLS - 1.0)
    table = np.maximum(1.0 - np.abs(source[:, None] - np.arange(CELLS, dtype=np.float32)[None, :]), 0.0)
    tables = []
    for j in (-1, 0, 1):
        moved = np.zeros_like(table)
        for q in range(BLK):
            if 0 <= q + j < BLK:
                moved[q] = table[q + j]
        tables.append((table[:, None, :, None] * moved[None, :, None, :]).reshape(BLK * BLK, CELLS * CELLS))
    return np.stack(tables)


def pyramid(tiles, rows, cols, features, image, blocks, routes, w_one, w_rates, w_depth, w_pool, w_proj,
            w_first, w_color, w_second, w_head):
    channels, width = w_one.shape
    cells = rows * cols
    per = CAP * CELLS * CELLS
    chunks = channels // CHUNK
    edge = REACH * cols
    held = routes.shape[0] // tiles * 8
    pixels = BLK * BLK
    whole = pl.BlockSpec(memory_space=pltpu.VMEM)
    away = pl.BlockSpec(memory_space=pl.ANY)
    dma = pltpu.SemaphoreType.DMA
    image = image.transpose(0, 2, 1).reshape(-1, image.shape[1])
    first, second = w_first.reshape(9 * width, width), w_second.reshape(9 * width, width)
    return pl.pallas_call(
        functools.partial(pyramid_kernel, tiles, rows, cols, channels, width),
        out_shape=(
            jax.ShapeDtypeStruct((cells, width), BF16),
            jax.ShapeDtypeStruct((1, width), F32),
            jax.ShapeDtypeStruct((held, pixels), BF16),
        ),
        in_specs=[away, away, away, whole, away, away, away, away, away, whole, whole, whole, whole, whole],
        out_specs=(whole, whole, whole),
        scratch_shapes=[
            pltpu.VMEM(image.shape, BF16),
            pltpu.VMEM(first.shape, BF16),
            pltpu.VMEM(second.shape, BF16),
            pltpu.VMEM((per, width), BF16),
            pltpu.VMEM((16, pixels), F32),
            pltpu.VMEM((pixels + 2 * BLK, 3 * width), BF16),
            pltpu.VMEM((pixels + 2 * BLK, 3 * width), BF16),
            pltpu.VMEM((pixels, 144), BF16),
            pltpu.VMEM((CAP * 8, pixels), F32),
            pltpu.VMEM((tiles * held, pixels), BF16),
            pltpu.VMEM((tiles, held, pixels), BF16),
            pltpu.VMEM((tiles * 16, pixels), BF16),
            dma((tiles,)),
            dma((tiles,)),
            pltpu.VMEM((cells, channels), BF16),
            pltpu.VMEM(w_one.shape, BF16),
            pltpu.VMEM(w_rates.shape, BF16),
            pltpu.VMEM(w_pool.shape, BF16),
            pltpu.VMEM(w_proj.shape, BF16),
            pltpu.VMEM((2, edge, channels), BF16),
            pltpu.VMEM((cells + 2 * edge, CHUNK), F32),
            pltpu.VMEM((3, cells, CHUNK), BF16),
            pltpu.VMEM((4, cells, width), F32),
            pltpu.VMEM((1, channels), F32),
            pltpu.VMEM((tiles, 1, channels), F32),
            pltpu.VMEM((tiles, per, width), BF16),
            pltpu.VMEM((tiles, per, width), BF16),
            pltpu.VMEM((tiles, 16, pixels), BF16),
            dma((8,)),
            dma((2, chunks)),
            dma((2, chunks)),
            dma((tiles,)),
            dma((tiles,)),
            dma((tiles,)),
            dma((tiles,)),
            dma((tiles,)),
            dma((tiles,)),
        ],
        compiler_params=pltpu.CompilerParams(collective_id=0, has_side_effects=True, vmem_limit_bytes=60 << 20),
        name="pyramid",
    )(
        features.reshape(cells, channels), w_one, w_rates, w_depth.transpose(1, 0, 2), w_pool, w_proj, image, first, second,
        w_color, w_head, jnp.asarray(upsample_tables(), BF16), blocks.T, routes.T,
    )


def shards(
    tiles,
    features,
    aerial_image,
    blocks,
    routes,
    w_one,
    w_depth,
    w_rates,
    w_pool,
    w_proj,
    w_first,
    w_color,
    w_second,
    w_head,
):
    rows, cols, channels = features.shape
    width = w_one.shape[1]
    aspp, context, refined = pyramid(
        tiles, rows, cols, features, aerial_image, blocks, routes, w_one, w_rates, w_depth, w_pool, w_proj,
        w_first[0], w_color[0], w_second[0], w_head[0],
    )
    refined = refined.reshape(-1, 8, BLK * BLK)[:, : w_head.shape[1], :]
    return aspp.reshape(rows, cols, width), context.reshape(width), refined


def solution(mesh):
    return jax.shard_map(
        functools.partial(shards, mesh.shape["tile"]),
        mesh=mesh,
        in_specs=(
            P(("groups", "tile"), None, None),
            P(None, ("groups", "tile"), None),
            P("groups", None),
            P("groups", None),
            P(),
            P(),
            P(),
            P(),
            P(),
            P("tile", None, None, None),
            P("tile", None, None),
            P("tile", None, None, None),
            P("tile", None, None),
        ),
        out_specs=(
            P(("groups", "tile"), None, None),
            P("groups"),
            P(("groups", "tile"), None, None),
        ),
        check_vma=False,
    )
```

time: 132 us -> 111 us (0.84); the launches traced: 129 us -> 111 us
  waiting for transfers between devices: 10.8 us -> 0 us
  Pallas kernels: 96.9 us -> 106 us
  starting transfers between devices: 6.47 us -> 0 us
  local copies, waits for them, and re-layouts: 9.48 us -> 4.38 us
  other arithmetic: 4.18 us -> 0 us
    pallas_call x1, Pallas kernels: 74.3 us -> 106 us  [pyramid(): pl.pallas_call(functools.partial(pyramid_kernel, tiles, rows, cols, chann...]
    pallas_call x1 -> x0, Pallas kernels: 22.5 us -> none  [refine(): pl.pallas_call(refine_kernel, out_shape=jax.ShapeDtypeStruct((CAP, 16, pi...]
    all_to_all x1 -> x0, waiting for transfers between devices: 10.8 us -> none  [shards(): lax.all_to_all(send_back.reshape(tiles, per_holder, result.shape[1], resu...]
    all_to_all x1 -> x0, starting transfers between devices: 6.47 us -> none  [shards(): lax.all_to_all(send_back.reshape(tiles, per_holder, result.shape[1], resu...]
    reshape x9 -> x0, local copies, waits for them, and re-layouts: 6.35 us -> none  [the longest x2 2.67 us: shards(): aerial_image.reshape(3, strip_blocks, BLK, across, BLK)]
    unnamed x17 -> x3, local copies, waits for them, and re-layouts: 1.95 us -> 4.38 us
    reduce_sum x2 -> x0, other arithmetic: 1.85 us -> none  [the longest x1 0.94 us: shards(): refined = jnp.sum(arrived, axis=0, dtype=F32).astype(BF16)]
  transfers between devices with their start and end apart: 1 -> 0, of which waited for: 1 -> 0; matrix products, arithmetic and copies ran while one was open for 0% -> 0% of each run, Pallas kernels for 0% -> 0%
where the time goes in v1:
time: 111 us
  Pallas kernels  106 us (95%)
  local copies, waits for them, and re-layouts  4.38 us (4%)
    pallas_call x1, Pallas kernels, pyramid(): pl.pallas_call(functools.partial(pyramid_kernel, tiles, rows, cols, chann...  106 us
    unnamed x3, local copies, waits for them, and re-layouts  4.38 us

profile of v1, /device:TPU:15, one launch (start us, length us, event | category | flops | bytes accessed | tf_op | source)
XLA Modules:
  0.0 110.8 jit_solution(2812309957315538576)
XLA Ops:
  0.6 105.7 %pyramid.1 = (bf16[768,256]{1,0:T(8,128)(2,1)}, f32[1,256]{1,0:T(1,128)}, bf16[16,1024]{1,0:T(8,128)(2,1)}) custom-call(bf16[768,2048]{1,0:T(8,128)(2,1)} %bitcast.15, bf16[2048,256]{1,0:T(8,128)(2,1)} %w_one_hbm.1, bf16[3,2048,256]{2,1,0:T(8,128)(2,1)} %w_rates_hbm.1, bf16[9,3,2048]{2,1,0:T(4,128)(2,1)} %bitcast.20, bf16[2048,256]{1,0:T(8,128)(2,1)} %w_pool_hbm.1, ...), custom_call_target="tpu_custom_call" | custom-call | tf_op jit(solution)/shard_map/pyramid/pallas_call | solution.py:479
  106.4 1.4 %copy.18 = bf16[2,6,1024]{2,0,1:T(2,128)(2,1)} copy(bf16[2,6,1024]{2,1,0:T(8,128)(2,1)} %bitcast.21) | data formatting | bytes 49152
  107.8 1.8 %copy.21 = bf16[32,24,256]{2,1,0:T(8,128)(2,1)} copy(bf16[32,24,256]{2,1,0:T(8,128)(2,1)} %bitcast.18) | data formatting | bytes 786432
  109.5 1.2 %copy.22 = f32[256]{0:T(256)} copy(f32[256]{0:T(256)} %bitcast.25) | data formatting | bytes 2048

commit v2 on v1

--- a/solution.py
+++ b/solution.py
@@ -13,7 +13,7 @@
 CELLS = 4
 RATES = (6, 12, 18)
 REACH = 18
-CHUNK = 256
+CHUNK = 512
 F32 = jnp.float32
 BF16 = jnp.bfloat16
 
@@ -247,7 +247,7 @@
                         total = term if total is None else total + term
                     return total
 
-                @pl.loop(0, rows // 2, unroll=2)
+                @pl.loop(0, rows // 2, unroll=4)
                 def _(pair, d=d, weigh=weigh, inner=inner, k=k):
                     results = []
                     for r in range(2):

time: 111 us -> 108 us (0.973)
  Pallas kernels: 106 us -> 103 us
    pallas_call x1, Pallas kernels: 106 us -> 103 us  [pyramid(): pl.pallas_call(functools.partial(pyramid_kernel, tiles, rows, cols, chann...]
where the time goes in v2:
time: 108 us
  Pallas kernels  103 us (95%)
  local copies, waits for them, and re-layouts  4.38 us (4%)
    pallas_call x1, Pallas kernels, pyramid(): pl.pallas_call(functools.partial(pyramid_kernel, tiles, rows, cols, chann...  103 us
    unnamed x3, local copies, waits for them, and re-layouts  4.38 us

profile of v2, /device:TPU:15, one launch (start us, length us, event | category | flops | bytes accessed | tf_op | source)
XLA Modules:
  0.0 108.0 jit_solution(982203688544052749)
XLA Ops:
  0.6 103.0 %pyramid.1 = (bf16[768,256]{1,0:T(8,128)(2,1)}, f32[1,256]{1,0:T(1,128)}, bf16[16,1024]{1,0:T(8,128)(2,1)}) custom-call(bf16[768,2048]{1,0:T(8,128)(2,1)} %bitcast.15, bf16[2048,256]{1,0:T(8,128)(2,1)} %w_one_hbm.1, bf16[3,2048,256]{2,1,0:T(8,128)(2,1)} %w_rates_hbm.1, bf16[9,3,2048]{2,1,0:T(4,128)(2,1)} %bitcast.20, bf16[2048,256]{1,0:T(8,128)(2,1)} %w_pool_hbm.1, ...), custom_call_target="tpu_custom_call" | custom-call | tf_op jit(solution)/shard_map/pyramid/pallas_call | solution.py:479
  103.6 1.4 %copy.18 = bf16[2,6,1024]{2,0,1:T(2,128)(2,1)} copy(bf16[2,6,1024]{2,1,0:T(8,128)(2,1)} %bitcast.21) | data formatting | bytes 49152
  105.0 1.8 %copy.21 = bf16[32,24,256]{2,1,0:T(8,128)(2,1)} copy(bf16[32,24,256]{2,1,0:T(8,128)(2,1)} %bitcast.18) | data formatting | bytes 786432
  106.8 1.2 %copy.22 = f32[256]{0:T(256)} copy(f32[256]{0:T(256)} %bitcast.25) | data formatting | bytes 2048
